TPU v7x, 256 devices: a whole 4x4x8 slice. The times are simulated.
256 devices in a mesh: grp: 8 (over y, core), dev: 32 (over z, x).
Axes of the slice: x: 4, y: 4, z: 8, core: 2. Of those that a mesh axis runs over, the one named last changes fastest.
Arguments:
- objective: float32 [8, 32, 1024, 256], P('grp', 'dev'), may hold values from -24 to 24
- schur: float32 [8, 32, 1024, 1024], P('grp', 'dev')
- local_inverse: float32 [8, 32, 1024, 1024], P('grp', 'dev')
- coarse_basis: float32 [8, 32, 64, 1024], P('grp', 'dev'), may hold values from -0.09375 to 0.09375
- coarse_inverse: float32 [8, 32, 32, 8192], P(None, 'dev', None, 'grp')
- stiffness: int32 [8, 32, 1024], P('grp', 'dev'), may hold values from 1 to 8
- face_rows: int32 [8, 32, 4, 256], P('grp', 'dev'), may hold values from -1 to 1023, as said below
- coarse_map: int32 [8, 32, 64], P('grp', 'dev'), may hold values from 0 to 255
Outputs:
- adjoint: float32 [8, 32, 1024, 256], P('grp', 'dev')
Inputs may be any that keep to these rules, and one draw needn't show every extreme that they name: `face_rows`: slot k of face p names the local row of the k-th row that the subdomain shares with its neighbour across face p, or -1; the live slots of a face come first, and the neighbour lists the same shared rows in the same order in its opposite face. The live slots of a subdomain name its rows 0 to n - 1 once each, n at most 1024, and at least one subdomain has all 1024 rows. Faces at the ends of the layout are empty; a face that joins two subdomains has 1 to 256 rows. `coarse_map`: entry e of subdomain (g, d) names the coarse dof (e // 32, d, e % 32), owned by the subdomain at grp index e // 32 of the same dev index.
All inputs are finite; a program needn't handle non-finite values.
Results may differ from a plain program's by a relative error of at most 0.0003.
Values sent between devices are 32-bit elements; how exact they have to be, the bound alone decides.
No kernel may reach another device: no remote copies, remote signals or barrier semaphores. Data moves between devices by JAX's collectives and lax.ppermute only.
A program may use at most 64 MiB of HBM per device.

v0:
```python
import jax
import jax.numpy as jnp
from jax import lax
from jax.sharding import PartitionSpec as P

INTERFACE = 1024
FACE_ROWS = 256
OWNED = 32
SWEEPS = 2


def padded(value, sides, width):
    for axis, dim in sides:
        size, length = (lax.axis_size(axis), value.shape[dim])
        up = [(i, (i + 1) % size) for i in range(size - 1)]
        down = [(j, i) for i, j in up]
        last = lax.slice_in_dim(value, length - width, length, axis=dim)
        initial = lax.slice_in_dim(value, 0, width, axis=dim)
        before = lax.ppermute(last, axis, up)
        after = lax.ppermute(initial, axis, down)
        value = jnp.concatenate([before, value, after], axis=dim)
    return value


def contract_first(left, right):
    return lax.dot_general(
        left,
        right,
        (((0,), (0,)), ((), ())),
        precision=lax.Precision.HIGHEST,
        preferred_element_type=jnp.float32,
    )


def on_device(
    objective, schur, local_inverse, coarse_basis, coarse_inverse, stiffness, face_rows, coarse_map
):
    highest = lax.Precision.HIGHEST
    schur_block = schur[0, 0]
    local_block = local_inverse[0, 0]
    basis_rows = coarse_basis[0, 0]
    inverse_tile = coarse_inverse.reshape(-1, coarse_inverse.shape[3])
    slot_rows = face_rows[0, 0]
    local_map = coarse_map[0, 0]
    gradient = objective[0, 0]
    slot_count = 4 * FACE_ROWS
    slot_index = jnp.where(slot_rows < 0, INTERFACE, slot_rows).reshape(-1)
    empty_map = jnp.full((INTERFACE,), slot_count, jnp.int32)
    inverse = empty_map.at[slot_index].set(jnp.arange(slot_count, dtype=jnp.int32), mode="drop")
    live_rows = (inverse < slot_count).astype(jnp.float32)[:, None]

    def neighbour(values):
        packed = jnp.take(values, slot_index, axis=0, mode="fill", fill_value=0)
        packed = packed.reshape(4, FACE_ROWS, values.shape[-1])
        packet = jnp.stack([jnp.stack([packed[2], packed[1]]), jnp.stack([packed[0], packed[3]])])
        extended = padded(packet, (("grp", 0), ("dev", 1)), 1)
        received = jnp.stack([extended[1, 0], extended[2, 3], extended[0, 2], extended[3, 1]])
        received = received.reshape(slot_count, values.shape[-1])
        return jnp.take(received, inverse, axis=0, mode="fill", fill_value=0)

    multiplicity = stiffness[0, 0].astype(jnp.float32)[:, None]
    weight = live_rows * multiplicity / (multiplicity + neighbour(multiplicity))
    column_rows = inverse_tile.shape[0]
    onehot = (local_map[:, None] == jnp.arange(column_rows, dtype=jnp.int32)[None, :]).astype(
        jnp.float32
    )
    dev_position = lax.axis_index("dev")
    adjoint = jnp.zeros(gradient.shape, jnp.float32)
    for sweep_index in range(SWEEPS):
        if sweep_index == 0:
            remain = gradient
        else:
            remain = gradient - contract_first(schur_block, adjoint)
        residual = live_rows * (remain + neighbour(remain))
        weighted = weight * residual
        local_terms = jnp.dot(
            basis_rows, weighted, precision=highest, preferred_element_type=jnp.float32
        )
        spread_terms = contract_first(onehot, local_terms)
        column_residual = lax.psum(spread_terms, "grp")
        partial_sums = contract_first(inverse_tile, column_residual)
        summed = lax.psum(partial_sums, "dev")
        owned_part = lax.dynamic_slice_in_dim(summed, dev_position * OWNED, OWNED, 0)
        column_solution = lax.all_gather(owned_part, "grp", axis=0, tiled=True)
        local_solution = jnp.dot(
            onehot, column_solution, precision=highest, preferred_element_type=jnp.float32
        )
        correction = contract_first(basis_rows, local_solution)
        update = weight * (contract_first(local_block, weighted) + correction)
        adjoint = adjoint + update + neighbour(update)
    return adjoint[None, None]


def solution(mesh):
    return jax.shard_map(
        on_device,
        mesh=mesh,
        in_specs=(
            P("grp", "dev", None, None),
            P("grp", "dev", None, None),
            P("grp", "dev", None, None),
            P("grp", "dev", None, None),
            P(None, "dev", None, "grp"),
            P("grp", "dev", None),
            P("grp", "dev", None, None),
            P("grp", "dev", None),
        ),
        out_specs=P("grp", "dev", None, None),
        check_vma=False,
    )
```

profile of v0, /device:TPU:14, one launch (start us, length us, event | category | flops | bytes accessed | tf_op | source)
XLA Modules:
  0.0 766.2 jit_solution(6774467022367490812)
XLA Ops:
  41.0 5.8 collective-permute-start.6
  55.4 15.2 %collective-permute-done.6 = f32[4,1,256,256]{3,2,1,0:T(8,128)} collective-permute-done((f32[4,1,256,256]{3,2,1,0:T(8,128)}, f32[4,1,256,256]{3,2,1,0:T(8,128)}, u32[]{:S(2)}, u32[]{:S(2)}) %collective-permute-start.6) | collective-permute-done | bytes 1048608 | tf_op jit(solution)/shard_map/ppermute | solution.py:19
  71.5 9.8 %collective-permute-done.7 = f32[4,1,256,256]{3,2,1,0:T(8,128)S(1)} collective-permute-done((f32[4,1,256,256]{3,2,1,0:T(8,128)S(1)}, f32[4,1,256,256]{3,2,1,0:T(8,128)S(1)}, u32[]{:S(2)}, u32[]{:S(2)}) %collective-permute-start.7) | collective-permute-done | bytes 1048608 | tf_op jit(solution)/shard_map/ppermute | solution.py:20
  81.4 4.7 gather_fusion.3
  90.1 66.4 %all-reduce.5.cloned.1.call-done = f32[256,256]{1,0:T(8,128)} async-done(((f32[256,256]{1,0:T(8,128)}), f32[256,256]{1,0:T(8,128)}) %all-reduce.5.cloned.1.call-update) | async-done | bytes 262160 | tf_op jit(solution)/shard_map/psum | solution.py:80
  159.5 150.0 %all-reduce.7.cloned.1.call-done = f32[1024,256]{0,1:T(8,128)} async-done(((f32[1024,256]{0,1:T(8,128)}), f32[1024,256]{0,1:T(8,128)}) %all-reduce.7.cloned.1.call-update) | async-done | bytes 1048592 | tf_op jit(solution)/shard_map/psum | solution.py:82
  311.2 13.3 %all_gather.6 = f32[256,256]{1,0:T(8,128)S(1)} all-gather(f32[32,256]{1,0:T(8,128)} %copy.36), channel_id=1, replica_groups=mesh['grp'=8,'dev'=32] {'grp'}, dimensions={0}, use_global_device_ids=true | all-gather | bytes 294912 | tf_op jit(solution)/shard_map/all_gather | solution.py:84
  326.4 6.9 fusion.12
  334.9 4.7 gather_fusion.4
  345.8 4.7 collective-permute-done.9
  360.6 19.8 %collective-permute-done.10 = f32[4,1,256,256]{3,2,1,0:T(8,128)S(1)} collective-permute-done((f32[4,1,256,256]{3,2,1,0:T(8,128)S(1)}, f32[4,1,256,256]{3,2,1,0:T(8,128)S(1)}, u32[]{:S(2)}, u32[]{:S(2)}) %collective-permute-start.10) | collective-permute-done | bytes 1048608 | tf_op jit(solution)/shard_map/ppermute | solution.py:19
  380.4 5.8 collective-permute-done.11
  386.4 4.7 gather_fusion.5
  393.6 6.4 fusion.27
  400.4 4.7 gather_fusion.6
  425.5 19.1 %collective-permute-done.14 = f32[4,1,256,256]{3,2,1,0:T(8,128)S(1)} collective-permute-done((f32[4,1,256,256]{3,2,1,0:T(8,128)S(1)}, f32[4,1,256,256]{3,2,1,0:T(8,128)S(1)}, u32[]{:S(2)}, u32[]{:S(2)}) %collective-permute-start.14) | collective-permute-done | bytes 1048608 | tf_op jit(solution)/shard_map/ppermute | solution.py:19
  448.7 4.7 gather_fusion.7
  457.3 62.6 %all-reduce.9.cloned.1.call-done = f32[256,256]{1,0:T(8,128)} async-done(((f32[256,256]{1,0:T(8,128)}), f32[256,256]{1,0:T(8,128)}) %all-reduce.9.cloned.1.call-update) | async-done | bytes 262160 | tf_op jit(solution)/shard_map/psum | solution.py:80
  523.0 149.5 %all-reduce.11.cloned.1.call-done = f32[1024,256]{0,1:T(8,128)} async-done(((f32[1024,256]{0,1:T(8,128)}), f32[1024,256]{0,1:T(8,128)}) %all-reduce.11.cloned.1.call-update) | async-done | bytes 1048592 | tf_op jit(solution)/shard_map/psum | solution.py:82
  674.1 13.1 %all_gather.7 = f32[256,256]{1,0:T(8,128)S(1)} all-gather(f32[32,256]{1,0:T(8,128)} %copy.41), channel_id=1, replica_groups=mesh['grp'=8,'dev'=32] {'grp'}, dimensions={0}, use_global_device_ids=true | all-gather | bytes 294912 | tf_op jit(solution)/shard_map/all_gather | solution.py:84
  689.2 6.9 fusion.21
  706.2 4.7 collective-permute-done.17
  721.1 19.8 %collective-permute-done.18 = f32[4,1,256,256]{3,2,1,0:T(8,128)S(1)} collective-permute-done((f32[4,1,256,256]{3,2,1,0:T(8,128)S(1)}, f32[4,1,256,256]{3,2,1,0:T(8,128)S(1)}, u32[]{:S(2)}, u32[]{:S(2)}) %collective-permute-start.18) | collective-permute-done | bytes 1048608 | tf_op jit(solution)/shard_map/ppermute | solution.py:19
  740.8 5.8 collective-permute-done.19
  (163 shorter events, 143.1 us)
Async XLA Ops:
  6.5 149.9 %all-reduce.5.cloned.1.call-start = ((), (), s32[]{:S(2)}) async-start(), calls=%async_computation | async-start | bytes 524288 | tf_op jit(solution)/shard_map/psum | solution.py:80
  12.6 19.6 %collective-permute-start.1 = (f32[1,2,256,1]{2,1,3,0:T(2,128)S(1)}, f32[1,2,256,1]{2,1,3,0:T(2,128)S(1)}, u32[]{:S(2)}, u32[]{:S(2)}) collective-permute-start(f32[1,2,256,1]{2,1,3,0:T(2,128)S(1)} %maximum_bitcast_fusion.9), channel_id=1, source_target_pairs={{32,0},{64,32},{96,64},{128,96},{160,128},{192,160},{224,192},{33,... | collective-permute-start | bytes 6152 | tf_op jit(solution)/shard_map/ppermute | solution.py:20
  14.5 17.7 %collective-permute-start = (f32[1,2,256,1]{2,1,3,0:T(2,128)S(1)}, f32[1,2,256,1]{2,1,3,0:T(2,128)S(1)}, u32[]{:S(2)}, u32[]{:S(2)}) collective-permute-start(f32[1,2,256,1]{2,1,3,0:T(2,128)S(1)} %maximum_bitcast_fusion.8), channel_id=1, source_target_pairs={{0,32},{32,64},{64,96},{96,128},{128,160},{160,192},{192,224},{1,3... | collective-permute-start | bytes 6152 | tf_op jit(solution)/shard_map/ppermute | solution.py:19
  21.6 16.6 %collective-permute-start.5 = (f32[1,2,256,256]{3,2,1,0:T(8,128)}, f32[1,2,256,256]{3,2,1,0:T(8,128)}, u32[]{:S(2)}, u32[]{:S(2)}) collective-permute-start(f32[1,2,256,256]{3,2,1,0:T(8,128)} %maximum_bitcast_fusion.1), channel_id=1, source_target_pairs={{32,0},{64,32},{96,64},{128,96},{160,128},{192,160},{224,192},{33,... | collective-permute-start | bytes 1572872 | tf_op jit(solution)/shard_map/ppermute | solution.py:20
  25.6 12.6 %collective-permute-start.4 = (f32[1,2,256,256]{3,2,1,0:T(8,128)}, f32[1,2,256,256]{3,2,1,0:T(8,128)}, u32[]{:S(2)}, u32[]{:S(2)}) collective-permute-start(f32[1,2,256,256]{3,2,1,0:T(8,128)} %maximum_bitcast_fusion), channel_id=1, source_target_pairs={{0,32},{32,64},{64,96},{96,128},{128,160},{160,192},{192,224},{1,3... | collective-permute-start | bytes 1572872 | tf_op jit(solution)/shard_map/ppermute | solution.py:19
  32.3 5.9 collective-permute-start.2
  36.0 10.8 %collective-permute-start.3 = (f32[4,1,256,1]{2,1,3,0:T(1,128)S(1)}, f32[4,1,256,1]{2,1,3,0:T(1,128)S(1)}, u32[]{:S(2)}, u32[]{:S(2)}) collective-permute-start(f32[4,1,256,1]{2,1,3,0:T(1,128)S(1)} %get-tuple-element.38), channel_id=1, source_target_pairs={{1,0},{2,1},{3,2},{4,3},{5,4},{6,5},{7,6},{8,7},{9,8},{10,9},{11,1... | collective-permute-start | bytes 12296 | tf_op jit(solution)/shard_map/ppermute | solution.py:20
  41.0 29.5 %collective-permute-start.6 = (f32[4,1,256,256]{3,2,1,0:T(8,128)}, f32[4,1,256,256]{3,2,1,0:T(8,128)}, u32[]{:S(2)}, u32[]{:S(2)}) collective-permute-start(f32[4,1,256,256]{3,2,1,0:T(8,128)} %get-tuple-element.19), channel_id=1, source_target_pairs={{0,1},{1,2},{2,3},{3,4},{4,5},{5,6},{6,7},{7,8},{8,9},{9,10},{10,1... | collective-permute-start | bytes 3145736 | tf_op jit(solution)/shard_map/ppermute | solution.py:19
  51.4 29.9 %collective-permute-start.7 = (f32[4,1,256,256]{3,2,1,0:T(8,128)S(1)}, f32[4,1,256,256]{3,2,1,0:T(8,128)S(1)}, u32[]{:S(2)}, u32[]{:S(2)}) collective-permute-start(f32[4,1,256,256]{3,2,1,0:T(8,128)S(1)} %get-tuple-element.20), channel_id=1, source_target_pairs={{1,0},{2,1},{3,2},{4,3},{5,4},{6,5},{7,6},{8,7},{9,8},{10,9},{11,1... | collective-permute-start | bytes 3145736 | tf_op jit(solution)/shard_map/ppermute | solution.py:20
  90.0 219.4 %all-reduce.7.cloned.1.call-start = ((), (), s32[]{:S(2)}) async-start(), calls=%async_computation.1 | async-start | bytes 2097152 | tf_op jit(solution)/shard_map/psum | solution.py:82
  159.4 360.6 %all-reduce.9.cloned.1.call-start = ((), (), s32[]{:S(2)}) async-start(), calls=%async_computation.2 | async-start | bytes 524288 | tf_op jit(solution)/shard_map/psum | solution.py:80
  341.1 9.4 %collective-permute-start.9 = (f32[1,2,256,256]{3,2,1,0:T(8,128)S(1)}, f32[1,2,256,256]{3,2,1,0:T(8,128)S(1)}, u32[]{:S(2)}, u32[]{:S(2)}) collective-permute-start(f32[1,2,256,256]{3,2,1,0:T(8,128)S(1)} %maximum_bitcast_fusion.3), channel_id=1, source_target_pairs={{32,0},{64,32},{96,64},{128,96},{160,128},{192,160},{224,192},{33,... | collective-permute-start | bytes 1572872 | tf_op jit(solution)/shard_map/ppermute | solution.py:20
  343.9 10.5 %collective-permute-start.8 = (f32[1,2,256,256]{3,2,1,0:T(8,128)S(1)}, f32[1,2,256,256]{3,2,1,0:T(8,128)S(1)}, u32[]{:S(2)}, u32[]{:S(2)}) collective-permute-start(f32[1,2,256,256]{3,2,1,0:T(8,128)S(1)} %maximum_bitcast_fusion.2), channel_id=1, source_target_pairs={{0,32},{32,64},{64,96},{96,128},{128,160},{160,192},{192,224},{1,3... | collective-permute-start | bytes 1572872 | tf_op jit(solution)/shard_map/ppermute | solution.py:19
  354.6 25.8 %collective-permute-start.10 = (f32[4,1,256,256]{3,2,1,0:T(8,128)S(1)}, f32[4,1,256,256]{3,2,1,0:T(8,128)S(1)}, u32[]{:S(2)}, u32[]{:S(2)}) collective-permute-start(f32[4,1,256,256]{3,2,1,0:T(8,128)S(1)} %get-tuple-element.17), channel_id=1, source_target_pairs={{0,1},{1,2},{2,3},{3,4},{4,5},{5,6},{6,7},{7,8},{8,9},{9,10},{10,1... | collective-permute-start | bytes 3145736 | tf_op jit(solution)/shard_map/ppermute | solution.py:19
  358.7 27.6 %collective-permute-start.11 = (f32[4,1,256,256]{3,2,1,0:T(8,128)S(1)}, f32[4,1,256,256]{3,2,1,0:T(8,128)S(1)}, u32[]{:S(2)}, u32[]{:S(2)}) collective-permute-start(f32[4,1,256,256]{3,2,1,0:T(8,128)S(1)} %get-tuple-element.18), channel_id=1, source_target_pairs={{1,0},{2,1},{3,2},{4,3},{5,4},{6,5},{7,6},{8,7},{9,8},{10,9},{11,1... | collective-permute-start | bytes 3145736 | tf_op jit(solution)/shard_map/ppermute | solution.py:20
  406.6 8.6 %collective-permute-start.13 = (f32[1,2,256,256]{3,2,1,0:T(8,128)S(1)}, f32[1,2,256,256]{3,2,1,0:T(8,128)S(1)}, u32[]{:S(2)}, u32[]{:S(2)}) collective-permute-start(f32[1,2,256,256]{3,2,1,0:T(8,128)S(1)} %maximum_bitcast_fusion.5), channel_id=1, source_target_pairs={{32,0},{64,32},{96,64},{128,96},{160,128},{192,160},{224,192},{33,... | collective-permute-start | bytes 1572872 | tf_op jit(solution)/shard_map/ppermute | solution.py:20
  408.6 10.5 %collective-permute-start.12 = (f32[1,2,256,256]{3,2,1,0:T(8,128)S(1)}, f32[1,2,256,256]{3,2,1,0:T(8,128)S(1)}, u32[]{:S(2)}, u32[]{:S(2)}) collective-permute-start(f32[1,2,256,256]{3,2,1,0:T(8,128)S(1)} %maximum_bitcast_fusion.4), channel_id=1, source_target_pairs={{0,32},{32,64},{64,96},{96,128},{128,160},{160,192},{192,224},{1,3... | collective-permute-start | bytes 1572872 | tf_op jit(solution)/shard_map/ppermute | solution.py:19
  419.3 25.3 %collective-permute-start.14 = (f32[4,1,256,256]{3,2,1,0:T(8,128)S(1)}, f32[4,1,256,256]{3,2,1,0:T(8,128)S(1)}, u32[]{:S(2)}, u32[]{:S(2)}) collective-permute-start(f32[4,1,256,256]{3,2,1,0:T(8,128)S(1)} %get-tuple-element.15), channel_id=1, source_target_pairs={{0,1},{1,2},{2,3},{3,4},{4,5},{5,6},{6,7},{7,8},{8,9},{9,10},{10,1... | collective-permute-start | bytes 3145736 | tf_op jit(solution)/shard_map/ppermute | solution.py:19
  421.3 27.4 %collective-permute-start.15 = (f32[4,1,256,256]{3,2,1,0:T(8,128)S(1)}, f32[4,1,256,256]{3,2,1,0:T(8,128)S(1)}, u32[]{:S(2)}, u32[]{:S(2)}) collective-permute-start(f32[4,1,256,256]{3,2,1,0:T(8,128)S(1)} %get-tuple-element.16), channel_id=1, source_target_pairs={{1,0},{2,1},{3,2},{4,3},{5,4},{6,5},{7,6},{8,7},{9,8},{10,9},{11,1... | collective-permute-start | bytes 3145736 | tf_op jit(solution)/shard_map/ppermute | solution.py:20
  457.3 215.2 %all-reduce.11.cloned.1.call-start = ((), (), s32[]{:S(2)}) async-start(), calls=%async_computation.3 | async-start | bytes 2097152 | tf_op jit(solution)/shard_map/psum | solution.py:82
  701.5 9.4 %collective-permute-start.17 = (f32[1,2,256,256]{3,2,1,0:T(8,128)S(1)}, f32[1,2,256,256]{3,2,1,0:T(8,128)S(1)}, u32[]{:S(2)}, u32[]{:S(2)}) collective-permute-start(f32[1,2,256,256]{3,2,1,0:T(8,128)S(1)} %maximum_bitcast_fusion.7), channel_id=1, source_target_pairs={{32,0},{64,32},{96,64},{128,96},{160,128},{192,160},{224,192},{33,... | collective-permute-start | bytes 1572872 | tf_op jit(solution)/shard_map/ppermute | solution.py:20
  704.3 10.5 %collective-permute-start.16 = (f32[1,2,256,256]{3,2,1,0:T(8,128)S(1)}, f32[1,2,256,256]{3,2,1,0:T(8,128)S(1)}, u32[]{:S(2)}, u32[]{:S(2)}) collective-permute-start(f32[1,2,256,256]{3,2,1,0:T(8,128)S(1)} %maximum_bitcast_fusion.6), channel_id=1, source_target_pairs={{0,32},{32,64},{64,96},{96,128},{128,160},{160,192},{192,224},{1,3... | collective-permute-start | bytes 1572872 | tf_op jit(solution)/shard_map/ppermute | solution.py:19
  715.0 25.8 %collective-permute-start.18 = (f32[4,1,256,256]{3,2,1,0:T(8,128)S(1)}, f32[4,1,256,256]{3,2,1,0:T(8,128)S(1)}, u32[]{:S(2)}, u32[]{:S(2)}) collective-permute-start(f32[4,1,256,256]{3,2,1,0:T(8,128)S(1)} %get-tuple-element.13), channel_id=1, source_target_pairs={{0,1},{1,2},{2,3},{3,4},{4,5},{5,6},{6,7},{7,8},{8,9},{9,10},{10,1... | collective-permute-start | bytes 3145736 | tf_op jit(solution)/shard_map/ppermute | solution.py:19
  719.1 27.6 %collective-permute-start.19 = (f32[4,1,256,256]{3,2,1,0:T(8,128)S(1)}, f32[4,1,256,256]{3,2,1,0:T(8,128)S(1)}, u32[]{:S(2)}, u32[]{:S(2)}) collective-permute-start(f32[4,1,256,256]{3,2,1,0:T(8,128)S(1)} %get-tuple-element.14), channel_id=1, source_target_pairs={{1,0},{2,1},{3,2},{4,3},{5,4},{6,5},{7,6},{8,7},{9,8},{10,9},{11,1... | collective-permute-start | bytes 3145736 | tf_op jit(solution)/shard_map/ppermute | solution.py:20
  (15 other events, 245.1 us)
Sparse Core Ops, SparseCore 0:
  90.1 66.2 all-reduce.4
  160.3 149.1 all-reduce.6
  457.4 62.5 all-reduce.8
  523.3 149.1 all-reduce.10
where the time goes:
time: 767 us; the launch traced here: 766 us
  waiting for transfers between devices  553 us (72%)
  local copies, waits for them, and re-layouts  72.2 us (9%)
  starting transfers between devices  54.6 us (7%)
  matrix products  34.6 us (5%)
  blocking collectives  26.3 us (3%)
  between operations  14 us (2%)
  other arithmetic  11.2 us (1%)
    psum x2, waiting for transfers between devices, on_device(): summed = lax.psum(partial_sums, 'dev')  300 us
    psum x2, waiting for transfers between devices, on_device(): column_residual = lax.psum(spread_terms, 'grp')  129 us
    ppermute x10, waiting for transfers between devices, padded(): before = lax.ppermute(last, axis, up)  85.5 us
    ppermute x10, waiting for transfers between devices, padded(): after = lax.ppermute(initial, axis, down)  39.2 us
    gather x9, local copies, waits for them, and re-layouts, neighbour(): return jnp.take(received, inverse, axis=0, mode='fill', fill_value=0)  31.6 us
    dot_general x9, matrix products, contract_first(): lax.dot_general(left, right, (((0,), (0,)), ((), ())), precision=lax.Prec...  30.5 us
    ppermute x10, starting transfers between devices, padded(): before = lax.ppermute(last, axis, up)  30.1 us
    all_gather x2, blocking collectives, on_device(): column_solution = lax.all_gather(owned_part, 'grp', axis=0, tiled=True)  26.3 us
  transfers between devices with their start and end apart: 24, of which 18 were waited for; matrix products, arithmetic and copies ran while one was open for 3% of the time, Pallas kernels for 0%

commit v1 on v0

--- a/solution.py
+++ b/solution.py
@@ -79,7 +79,7 @@
         spread_terms = contract_first(onehot, local_terms)
         column_residual = lax.psum(spread_terms, "grp")
         partial_sums = contract_first(inverse_tile, column_residual)
-        summed = lax.psum(partial_sums, "dev")
+        summed = jnp.sum(lax.all_gather(partial_sums, "dev"), axis=0)
         owned_part = lax.dynamic_slice_in_dim(summed, dev_position * OWNED, OWNED, 0)
         column_solution = lax.all_gather(owned_part, "grp", axis=0, tiled=True)
         local_solution = jnp.dot(

time: 767 us -> 1010 us (1.32)
  waiting for transfers between devices: 553 us -> 719 us
  local copies, waits for them, and re-layouts: 72.2 us -> 128 us
  other arithmetic: 11.2 us -> 26.3 us
    all_gather x0 -> x2, waiting for transfers between devices: none -> 466 us  [on_device(): summed = jnp.sum(lax.all_gather(partial_sums, 'dev'), axis=0)]
    psum x2 -> x0, waiting for transfers between devices: 300 us -> none  [on_device(): summed = lax.psum(partial_sums, 'dev')]
    unnamed x33 -> x35, local copies, waits for them, and re-layouts: 1.18 us -> 58.7 us
    reduce_sum x0 -> x2, other arithmetic: none -> 15.1 us  [on_device(): summed = jnp.sum(lax.all_gather(partial_sums, 'dev'), axis=0)]
  transfers between devices with their start and end apart: 24 -> 24, of which waited for: 18 -> 18; matrix products, arithmetic and copies ran while one was open for 3% -> 2% of each run, Pallas kernels for 0% -> 0%
where the time goes in v1:
time: 1010 us; the launch traced here: 1000 us
  waiting for transfers between devices  719 us (71%)
  local copies, waits for them, and re-layouts  128 us (13%)
  starting transfers between devices  54.4 us (5%)
  matrix products  34.6 us (3%)
  blocking collectives  26.8 us (3%)
  other arithmetic  26.3 us (3%)
  between operations  14.3 us (1%)
    all_gather x2, waiting for transfers between devices, on_device(): summed = jnp.sum(lax.all_gather(partial_sums, 'dev'), axis=0)  466 us
    psum x2, waiting for transfers between devices, on_device(): column_residual = lax.psum(spread_terms, 'grp')  130 us
    ppermute x10, waiting for transfers between devices, padded(): before = lax.ppermute(last, axis, up)  85.7 us
    unnamed x35, local copies, waits for them, and re-layouts  58.7 us
    ppermute x10, waiting for transfers between devices, padded(): after = lax.ppermute(initial, axis, down)  38.2 us
    gather x9, local copies, waits for them, and re-layouts, neighbour(): return jnp.take(received, inverse, axis=0, mode='fill', fill_value=0)  31.6 us
    dot_general x9, matrix products, contract_first(): lax.dot_general(left, right, (((0,), (0,)), ((), ())), precision=lax.Prec...  30.5 us
    ppermute x10, starting transfers between devices, padded(): before = lax.ppermute(last, axis, up)  29.1 us
  transfers between devices with their start and end apart: 24, of which 18 were waited for; matrix products, arithmetic and copies ran while one was open for 2% of the time, Pallas kernels for 0%

profile of v1, /device:TPU:14, one launch (start us, length us, event | category | flops | bytes accessed | tf_op | source)
XLA Modules:
  0.0 1003.7 jit_solution(3274192261730357233)
XLA Ops:
  41.0 5.8 collective-permute-start.6
  55.4 15.2 %collective-permute-done.6 = f32[4,1,256,256]{3,2,1,0:T(8,128)} collective-permute-done((f32[4,1,256,256]{3,2,1,0:T(8,128)}, f32[4,1,256,256]{3,2,1,0:T(8,128)}, u32[]{:S(2)}, u32[]{:S(2)}) %collective-permute-start.6) | collective-permute-done | bytes 1048608 | tf_op jit(solution)/shard_map/ppermute | solution.py:19
  71.5 9.8 collective-permute-done.7
  81.4 4.7 gather_fusion.3
  90.1 66.4 %all-reduce.3.cloned.1.call-done = f32[256,256]{1,0:T(8,128)} async-done(((f32[256,256]{1,0:T(8,128)}), f32[256,256]{1,0:T(8,128)}) %all-reduce.3.cloned.1.call-update) | async-done | bytes 262160 | tf_op jit(solution)/shard_map/psum | solution.py:80
  159.5 232.8 %all-gather.5.cloned.1.call-done = f32[32768,256]{0,1:T(8,128)} async-done(((f32[1024,256]{0,1:T(8,128)}), f32[32768,256]{0,1:T(8,128)}) %all-gather.5.cloned.1.call-update) | async-done | bytes 33554448 | tf_op jit(solution)/shard_map/all_gather | solution.py:82
  392.3 28.8 %copy.60 = f32[32,8,32,1024]{3,2,1,0:T(8,128)S(1)} copy(f32[32,8,32,1024]{3,1,2,0:T(8,128)} %bitcast.219) | data formatting | bytes 67108864
  421.1 7.6 bitcast_reduce_fusion.1
  429.5 13.5 %all_gather.20 = f32[256,256]{1,0:T(8,128)S(1)} all-gather(f32[32,256]{1,0:T(8,128)} %copy.48), channel_id=1, replica_groups=mesh['grp'=8,'dev'=32] {'grp'}, dimensions={0}, use_global_device_ids=true | all-gather | bytes 294912 | tf_op jit(solution)/shard_map/all_gather | solution.py:84
  444.9 6.9 fusion.12
  464.3 4.7 collective-permute-done.9
  479.1 19.9 %collective-permute-done.10 = f32[4,1,256,256]{3,2,1,0:T(8,128)S(1)} collective-permute-done((f32[4,1,256,256]{3,2,1,0:T(8,128)S(1)}, f32[4,1,256,256]{3,2,1,0:T(8,128)S(1)}, u32[]{:S(2)}, u32[]{:S(2)}) %collective-permute-start.10) | collective-permute-done | bytes 1048608 | tf_op jit(solution)/shard_map/ppermute | solution.py:19
  499.0 5.3 collective-permute-done.11
  511.7 6.4 fusion.27
  543.5 19.2 %collective-permute-done.14 = f32[4,1,256,256]{3,2,1,0:T(8,128)S(1)} collective-permute-done((f32[4,1,256,256]{3,2,1,0:T(8,128)S(1)}, f32[4,1,256,256]{3,2,1,0:T(8,128)S(1)}, u32[]{:S(2)}, u32[]{:S(2)}) %collective-permute-start.14) | collective-permute-done | bytes 1048608 | tf_op jit(solution)/shard_map/ppermute | solution.py:19
  575.4 63.4 %all-reduce.5.cloned.1.call-done = f32[256,256]{1,0:T(8,128)} async-done(((f32[256,256]{1,0:T(8,128)}), f32[256,256]{1,0:T(8,128)}) %all-reduce.5.cloned.1.call-update) | async-done | bytes 262160 | tf_op jit(solution)/shard_map/psum | solution.py:80
  641.8 232.9 %all-gather.7.cloned.1.call-done = f32[32768,256]{0,1:T(8,128)} async-done(((f32[1024,256]{0,1:T(8,128)}), f32[32768,256]{0,1:T(8,128)}) %all-gather.7.cloned.1.call-update) | async-done | bytes 33554448 | tf_op jit(solution)/shard_map/all_gather | solution.py:82
  874.6 28.8 %copy.61 = f32[32,8,32,1024]{3,2,1,0:T(8,128)S(1)} copy(f32[32,8,32,1024]{3,1,2,0:T(8,128)} %bitcast.220) | data formatting | bytes 67108864
  903.4 7.6 bitcast_reduce_fusion
  911.7 13.3 %all_gather.23 = f32[256,256]{1,0:T(8,128)S(1)} all-gather(f32[32,256]{1,0:T(8,128)} %copy.53), channel_id=1, replica_groups=mesh['grp'=8,'dev'=32] {'grp'}, dimensions={0}, use_global_device_ids=true | all-gather | bytes 294912 | tf_op jit(solution)/shard_map/all_gather | solution.py:84
  927.0 7.0 fusion.21
  944.0 4.7 collective-permute-done.17
  958.8 19.9 %collective-permute-done.18 = f32[4,1,256,256]{3,2,1,0:T(8,128)S(1)} collective-permute-done((f32[4,1,256,256]{3,2,1,0:T(8,128)S(1)}, f32[4,1,256,256]{3,2,1,0:T(8,128)S(1)}, u32[]{:S(2)}, u32[]{:S(2)}) %collective-permute-start.18) | collective-permute-done | bytes 1048608 | tf_op jit(solution)/shard_map/ppermute | solution.py:19
  978.7 5.3 collective-permute-done.19
  (167 shorter events, 159.7 us)
Async XLA Ops:
  6.5 149.9 %all-reduce.3.cloned.1.call-start = ((), (), s32[]{:S(2)}) async-start(), calls=%async_computation | async-start | bytes 524288 | tf_op jit(solution)/shard_map/psum | solution.py:80
  12.6 19.6 %collective-permute-start.1 = (f32[1,2,256,1]{2,1,3,0:T(2,128)S(1)}, f32[1,2,256,1]{2,1,3,0:T(2,128)S(1)}, u32[]{:S(2)}, u32[]{:S(2)}) collective-permute-start(f32[1,2,256,1]{2,1,3,0:T(2,128)S(1)} %maximum_bitcast_fusion.9), channel_id=1, source_target_pairs={{32,0},{64,32},{96,64},{128,96},{160,128},{192,160},{224,192},{33,... | collective-permute-start | bytes 6152 | tf_op jit(solution)/shard_map/ppermute | solution.py:20
  14.5 17.7 %collective-permute-start = (f32[1,2,256,1]{2,1,3,0:T(2,128)S(1)}, f32[1,2,256,1]{2,1,3,0:T(2,128)S(1)}, u32[]{:S(2)}, u32[]{:S(2)}) collective-permute-start(f32[1,2,256,1]{2,1,3,0:T(2,128)S(1)} %maximum_bitcast_fusion.8), channel_id=1, source_target_pairs={{0,32},{32,64},{64,96},{96,128},{128,160},{160,192},{192,224},{1,3... | collective-permute-start | bytes 6152 | tf_op jit(solution)/shard_map/ppermute | solution.py:19
  21.6 16.6 %collective-permute-start.5 = (f32[1,2,256,256]{3,2,1,0:T(8,128)}, f32[1,2,256,256]{3,2,1,0:T(8,128)}, u32[]{:S(2)}, u32[]{:S(2)}) collective-permute-start(f32[1,2,256,256]{3,2,1,0:T(8,128)} %maximum_bitcast_fusion.1), channel_id=1, source_target_pairs={{32,0},{64,32},{96,64},{128,96},{160,128},{192,160},{224,192},{33,... | collective-permute-start | bytes 1572872 | tf_op jit(solution)/shard_map/ppermute | solution.py:20
  25.6 12.6 %collective-permute-start.4 = (f32[1,2,256,256]{3,2,1,0:T(8,128)}, f32[1,2,256,256]{3,2,1,0:T(8,128)}, u32[]{:S(2)}, u32[]{:S(2)}) collective-permute-start(f32[1,2,256,256]{3,2,1,0:T(8,128)} %maximum_bitcast_fusion), channel_id=1, source_target_pairs={{0,32},{32,64},{64,96},{96,128},{128,160},{160,192},{192,224},{1,3... | collective-permute-start | bytes 1572872 | tf_op jit(solution)/shard_map/ppermute | solution.py:19
  32.3 5.9 collective-permute-start.2
  36.0 10.8 %collective-permute-start.3 = (f32[4,1,256,1]{2,1,3,0:T(1,128)S(1)}, f32[4,1,256,1]{2,1,3,0:T(1,128)S(1)}, u32[]{:S(2)}, u32[]{:S(2)}) collective-permute-start(f32[4,1,256,1]{2,1,3,0:T(1,128)S(1)} %get-tuple-element.38), channel_id=1, source_target_pairs={{1,0},{2,1},{3,2},{4,3},{5,4},{6,5},{7,6},{8,7},{9,8},{10,9},{11,1... | collective-permute-start | bytes 12296 | tf_op jit(solution)/shard_map/ppermute | solution.py:20
  41.0 29.5 %collective-permute-start.6 = (f32[4,1,256,256]{3,2,1,0:T(8,128)}, f32[4,1,256,256]{3,2,1,0:T(8,128)}, u32[]{:S(2)}, u32[]{:S(2)}) collective-permute-start(f32[4,1,256,256]{3,2,1,0:T(8,128)} %get-tuple-element.19), channel_id=1, source_target_pairs={{0,1},{1,2},{2,3},{3,4},{4,5},{5,6},{6,7},{7,8},{8,9},{9,10},{10,1... | collective-permute-start | bytes 3145736 | tf_op jit(solution)/shard_map/ppermute | solution.py:19
  51.4 29.9 %collective-permute-start.7 = (f32[4,1,256,256]{3,2,1,0:T(8,128)S(1)}, f32[4,1,256,256]{3,2,1,0:T(8,128)S(1)}, u32[]{:S(2)}, u32[]{:S(2)}) collective-permute-start(f32[4,1,256,256]{3,2,1,0:T(8,128)S(1)} %get-tuple-element.20), channel_id=1, source_target_pairs={{1,0},{2,1},{3,2},{4,3},{5,4},{6,5},{7,6},{8,7},{9,8},{10,9},{11,1... | collective-permute-start | bytes 3145736 | tf_op jit(solution)/shard_map/ppermute | solution.py:20
  90.0 302.3 %all-gather.5.cloned.1.call-start = ((), (), s32[]{:S(2)}) async-start(), calls=%async_computation.2 | async-start | bytes 34603008 | tf_op jit(solution)/shard_map/all_gather | solution.py:82
  159.5 479.3 %all-reduce.5.cloned.1.call-start = ((), (), s32[]{:S(2)}) async-start(), calls=%async_computation.1 | async-start | bytes 524288 | tf_op jit(solution)/shard_map/psum | solution.py:80
  459.7 9.4 collective-permute-start.9
  462.4 10.5 %collective-permute-start.8 = (f32[1,2,256,256]{3,2,1,0:T(8,128)S(1)}, f32[1,2,256,256]{3,2,1,0:T(8,128)S(1)}, u32[]{:S(2)}, u32[]{:S(2)}) collective-permute-start(f32[1,2,256,256]{3,2,1,0:T(8,128)S(1)} %maximum_bitcast_fusion.2), channel_id=1, source_target_pairs={{0,32},{32,64},{64,96},{96,128},{128,160},{160,192},{192,224},{1,3... | collective-permute-start | bytes 1572872 | tf_op jit(solution)/shard_map/ppermute | solution.py:19
  473.2 25.8 %collective-permute-start.10 = (f32[4,1,256,256]{3,2,1,0:T(8,128)S(1)}, f32[4,1,256,256]{3,2,1,0:T(8,128)S(1)}, u32[]{:S(2)}, u32[]{:S(2)}) collective-permute-start(f32[4,1,256,256]{3,2,1,0:T(8,128)S(1)} %get-tuple-element.17), channel_id=1, source_target_pairs={{0,1},{1,2},{2,3},{3,4},{4,5},{5,6},{6,7},{7,8},{8,9},{9,10},{10,1... | collective-permute-start | bytes 3145736 | tf_op jit(solution)/shard_map/ppermute | solution.py:19
  476.7 27.6 %collective-permute-start.11 = (f32[4,1,256,256]{3,2,1,0:T(8,128)S(1)}, f32[4,1,256,256]{3,2,1,0:T(8,128)S(1)}, u32[]{:S(2)}, u32[]{:S(2)}) collective-permute-start(f32[4,1,256,256]{3,2,1,0:T(8,128)S(1)} %get-tuple-element.18), channel_id=1, source_target_pairs={{1,0},{2,1},{3,2},{4,3},{5,4},{6,5},{7,6},{8,7},{9,8},{10,9},{11,1... | collective-permute-start | bytes 3145736 | tf_op jit(solution)/shard_map/ppermute | solution.py:20
  524.7 8.6 collective-permute-start.13
  526.6 10.5 %collective-permute-start.12 = (f32[1,2,256,256]{3,2,1,0:T(8,128)S(1)}, f32[1,2,256,256]{3,2,1,0:T(8,128)S(1)}, u32[]{:S(2)}, u32[]{:S(2)}) collective-permute-start(f32[1,2,256,256]{3,2,1,0:T(8,128)S(1)} %maximum_bitcast_fusion.4), channel_id=1, source_target_pairs={{0,32},{32,64},{64,96},{96,128},{128,160},{160,192},{192,224},{1,3... | collective-permute-start | bytes 1572872 | tf_op jit(solution)/shard_map/ppermute | solution.py:19
  537.4 25.3 %collective-permute-start.14 = (f32[4,1,256,256]{3,2,1,0:T(8,128)S(1)}, f32[4,1,256,256]{3,2,1,0:T(8,128)S(1)}, u32[]{:S(2)}, u32[]{:S(2)}) collective-permute-start(f32[4,1,256,256]{3,2,1,0:T(8,128)S(1)} %get-tuple-element.15), channel_id=1, source_target_pairs={{0,1},{1,2},{2,3},{3,4},{4,5},{5,6},{6,7},{7,8},{8,9},{9,10},{10,1... | collective-permute-start | bytes 3145736 | tf_op jit(solution)/shard_map/ppermute | solution.py:19
  539.3 27.4 %collective-permute-start.15 = (f32[4,1,256,256]{3,2,1,0:T(8,128)S(1)}, f32[4,1,256,256]{3,2,1,0:T(8,128)S(1)}, u32[]{:S(2)}, u32[]{:S(2)}) collective-permute-start(f32[4,1,256,256]{3,2,1,0:T(8,128)S(1)} %get-tuple-element.16), channel_id=1, source_target_pairs={{1,0},{2,1},{3,2},{4,3},{5,4},{6,5},{7,6},{8,7},{9,8},{10,9},{11,1... | collective-permute-start | bytes 3145736 | tf_op jit(solution)/shard_map/ppermute | solution.py:20
  575.4 299.3 %all-gather.7.cloned.1.call-start = ((), (), s32[]{:S(2)}) async-start(), calls=%async_computation.3 | async-start | bytes 34603008 | tf_op jit(solution)/shard_map/all_gather | solution.py:82
  939.3 9.4 collective-permute-start.17
  942.1 10.5 %collective-permute-start.16 = (f32[1,2,256,256]{3,2,1,0:T(8,128)S(1)}, f32[1,2,256,256]{3,2,1,0:T(8,128)S(1)}, u32[]{:S(2)}, u32[]{:S(2)}) collective-permute-start(f32[1,2,256,256]{3,2,1,0:T(8,128)S(1)} %maximum_bitcast_fusion.6), channel_id=1, source_target_pairs={{0,32},{32,64},{64,96},{96,128},{128,160},{160,192},{192,224},{1,3... | collective-permute-start | bytes 1572872 | tf_op jit(solution)/shard_map/ppermute | solution.py:19
  952.9 25.8 %collective-permute-start.18 = (f32[4,1,256,256]{3,2,1,0:T(8,128)S(1)}, f32[4,1,256,256]{3,2,1,0:T(8,128)S(1)}, u32[]{:S(2)}, u32[]{:S(2)}) collective-permute-start(f32[4,1,256,256]{3,2,1,0:T(8,128)S(1)} %get-tuple-element.13), channel_id=1, source_target_pairs={{0,1},{1,2},{2,3},{3,4},{4,5},{5,6},{6,7},{7,8},{8,9},{9,10},{10,1... | collective-permute-start | bytes 3145736 | tf_op jit(solution)/shard_map/ppermute | solution.py:19
  956.4 27.6 %collective-permute-start.19 = (f32[4,1,256,256]{3,2,1,0:T(8,128)S(1)}, f32[4,1,256,256]{3,2,1,0:T(8,128)S(1)}, u32[]{:S(2)}, u32[]{:S(2)}) collective-permute-start(f32[4,1,256,256]{3,2,1,0:T(8,128)S(1)} %get-tuple-element.14), channel_id=1, source_target_pairs={{1,0},{2,1},{3,2},{4,3},{5,4},{6,5},{7,6},{8,7},{9,8},{10,9},{11,1... | collective-permute-start | bytes 3145736 | tf_op jit(solution)/shard_map/ppermute | solution.py:20
  (15 other events, 245.1 us)
Sparse Core Ops, SparseCore 0:
  90.1 66.2 all-reduce.2
  159.6 232.6 all-gather.4
  575.5 63.2 all-reduce.4
  641.9 232.6 all-gather.6
